TPU v7x, 256 devices: a whole 4x4x8 slice. The times are simulated.
256 devices in a mesh: grp: 8 (over y, core), sub: 32 (over x, z).
Axes of the slice: x: 4, y: 4, z: 8, core: 2. Of those that a mesh axis runs over, the one named last changes fastest.
Arguments:
- cluster_pos: float32 [3, 4096], P(None, 'sub'), may hold values from -3 to 3
- cluster_vel: float32 [3, 4096], P(None, 'sub'), may hold values from -15 to 15
- cluster_mass: float32 [4096], P('sub'), may hold values from 3 to 60
- galaxy_pos: float32 [3, 131072], P(None, ('grp', 'sub')), may hold values from -1 to 7
- galaxy_vel: float32 [3, 131072], P(None, ('grp', 'sub')), may hold values from -3 to 3
- galaxy_kind: int32 [131072], P(('grp', 'sub')), may hold values from 0 to 3
- species_mass: float32 [4], replicated, may hold values from 10 to 80
Outputs:
- cluster_pos_out: float32 [3, 4096], P(None, 'sub')
- cluster_vel_out: float32 [3, 4096], P(None, 'sub')
- galaxy_pos_out: float32 [3, 131072], P(None, ('grp', 'sub'))
- galaxy_vel_out: float32 [3, 131072], P(None, ('grp', 'sub'))
All inputs are finite; a program needn't handle non-finite values.
Results may differ from a plain program's by a relative error of at most 0.0003.
Values sent between devices are 32-bit elements; how exact they have to be, the bound alone decides.
A program may use at most 64 MiB of HBM per device.

v0:
```python
import jax
import jax.numpy as jnp
from jax import lax
from jax.sharding import PartitionSpec as P

SUBSTEPS = 8
step_time = 0.5
bridge_soft = 0.01
cluster_soft = 0.0025
tile_limit = 524288


def pick_block(target_count, source_count):
    tile_size = target_count
    while tile_size > 1 and (
        tile_size * source_count > tile_limit or target_count % tile_size != 0
    ):
        tile_size = tile_size // 2
    return tile_size


def field(targets, sources, masses, soften):
    target_count = targets.shape[1]
    tile_size = pick_block(target_count, sources.shape[1])

    def field_one_tile(target_tile):
        separation = sources[:, None, :] - target_tile[:, :, None]
        distance = jnp.sum(separation * separation, axis=0) + soften
        inverse = lax.rsqrt(distance)
        weight = masses[None, :] * inverse * inverse * inverse
        return jnp.sum(separation * weight[None], axis=2)

    stacked = targets.reshape(3, target_count // tile_size, tile_size).transpose(1, 0, 2)
    result = lax.map(field_one_tile, stacked)
    return result.transpose(1, 0, 2).reshape(3, target_count)


def rates(target_pos, target_vel, source_pos, source_vel, masses, soften):
    target_count = target_pos.shape[1]
    tile_size = pick_block(target_count, source_pos.shape[1])

    def rates_one_tile(target_tile):
        separation = source_pos[:, None, :] - target_tile[:3, :, None]
        closing = source_vel[:, None, :] - target_tile[3:, :, None]
        distance = jnp.sum(separation * separation, axis=0) + soften
        inverse = lax.rsqrt(distance)
        weight = masses[None, :] * inverse * inverse * inverse
        radial = 3.0 * jnp.sum(separation * closing, axis=0) / distance
        acceleration = jnp.sum(separation * weight[None], axis=2)
        jerk_rate = jnp.sum((closing - radial[None] * separation) * weight[None], axis=2)
        return jnp.concatenate([acceleration, jerk_rate], axis=0)

    stacked = jnp.concatenate([target_pos, target_vel], axis=0)
    stacked = stacked.reshape(6, target_count // tile_size, tile_size).transpose(1, 0, 2)
    result = lax.map(rates_one_tile, stacked)
    return result.transpose(1, 0, 2).reshape(6, target_count)


def local(
    cluster_pos, cluster_vel, cluster_mass, galaxy_pos, galaxy_vel, galaxy_kind, species_mass
):
    star_count = cluster_pos.shape[1]
    member_count = lax.axis_size("sub")
    group_count = lax.axis_size("grp")
    total_stars = star_count * member_count
    total_bodies = galaxy_pos.shape[1] * member_count * group_count
    star_mass = cluster_mass / total_stars
    species = jnp.arange(species_mass.shape[0], dtype=jnp.int32)
    body_mass = (
        jnp.sum(
            jnp.where(galaxy_kind[None, :] == species[:, None], species_mass[:, None], 0.0), axis=0
        )
        / total_bodies
    )
    half_step = step_time / 2.0

    def kick(star_positions, body_positions):
        stacked = jnp.concatenate([star_positions, star_mass[None, :]], axis=0)
        gathered = lax.all_gather(stacked, "sub", axis=1, tiled=True)
        galaxy_push = field(body_positions, gathered[:3], gathered[3], bridge_soft)
        partial_value = field(gathered[:3], body_positions, body_mass, bridge_soft)
        summed = lax.psum(partial_value, ("grp", "sub"))
        cluster_pull = lax.dynamic_slice_in_dim(
            summed, lax.axis_index("sub") * star_count, star_count, 1
        )
        return (cluster_pull, galaxy_push)

    def evaluate(guess_pos, guess_vel):
        sources = jnp.concatenate([guess_pos, guess_vel, star_mass[None, :]], axis=0)
        target_pos, target_vel = (guess_pos, guess_vel)
        source_piece = lax.all_gather(sources, "sub", axis=1, tiled=True)
        result = rates(
            target_pos,
            target_vel,
            source_piece[:3],
            source_piece[3:6],
            source_piece[6],
            cluster_soft,
        )
        return (result[:3], result[3:])

    first_pull, first_push = kick(cluster_pos, galaxy_pos)
    star_vel = cluster_vel + half_step * first_pull
    body_vel = galaxy_vel + half_step * first_push
    body_pos = galaxy_pos + step_time * body_vel
    substep_time = step_time / SUBSTEPS
    positions, velocity = (cluster_pos, star_vel)
    acceleration, jerk_rate = evaluate(positions, velocity)
    for substep in range(SUBSTEPS):
        guess_pos = positions + substep_time * (
            velocity + substep_time * (acceleration / 2.0 + substep_time * jerk_rate / 6.0)
        )
        guess_vel = velocity + substep_time * (acceleration + substep_time * jerk_rate / 2.0)
        new_acc, new_jerk = evaluate(guess_pos, guess_vel)
        new_vel = (
            velocity
            + substep_time / 2.0 * (acceleration + new_acc)
            + substep_time * substep_time / 12.0 * (jerk_rate - new_jerk)
        )
        new_pos = (
            positions
            + substep_time / 2.0 * (velocity + new_vel)
            + substep_time * substep_time / 12.0 * (acceleration - new_acc)
        )
        positions, velocity, acceleration, jerk_rate = (new_pos, new_vel, new_acc, new_jerk)
    second_pull, second_push = kick(positions, body_pos)
    return (
        positions,
        velocity + half_step * second_pull,
        body_pos,
        body_vel + half_step * second_push,
    )


def solution(mesh):
    return jax.shard_map(
        local,
        mesh=mesh,
        in_specs=(
            P(None, "sub"),
            P(None, "sub"),
            P("sub"),
            P(None, ("grp", "sub")),
            P(None, ("grp", "sub")),
            P(("grp", "sub")),
            P(),
        ),
        out_specs=(
            P(None, "sub"),
            P(None, "sub"),
            P(None, ("grp", "sub")),
            P(None, ("grp", "sub")),
        ),
        check_vma=False,
    )
```

profile of v0, /device:TPU:1, one launch (start us, length us, event | category | flops | bytes accessed | tf_op | source)
XLA Modules:
  0.0 715.4 jit_solution(4176489332510097580)
XLA Ops:
  2.0 40.5 %all_gather.33 = f32[4,4096]{1,0:T(4,128)S(1)} all-gather(f32[4,128]{1,0:T(4,128)S(1)} %pad_maximum_fusion.10), channel_id=1, replica_groups=mesh['grp'=8,'sub'=32] {'sub'}, dimensions={1}, use_global_device_ids=true | all-gather | bytes 67584 | tf_op jit(solution)/shard_map/all_gather | solution.py:79
  43.3 14.5 %while.8 = (s32[]{:T(128)}, f32[4,3,1024]{2,1,0:T(4,128)S(1)}, f32[3,512]{1,0:T(4,128)}, f32[4,3,1024]{2,1,0:T(4,128)S(1)}, f32[512]{0:T(512)S(1)}, /*index=5*/s32[]{:T(128)}) while((s32[]{:T(128)}, f32[4,3,1024]{2,1,0:T(4,128)S(1)}, f32[3,512]{1,0:T(4,128)}, f32[4,3,1024]{2,1,0:T(4,128)S(1)}, f32[512]{0:T(512)S(1)}, ...), condition=%wide.region_4.5_spmd, body=%wide.region_1.4_spmd.sunk | while | flops 11006978 | bytes 8521833 | solution.py:34
  43.3 1.6 fusion.70
  45.6 1.2 fusion.71
  46.9 1.6 fusion.70
  49.3 1.2 fusion.71
  50.5 1.6 fusion.70
  52.9 1.2 fusion.71
  54.2 1.6 fusion.70
  56.5 1.2 fusion.71
  57.8 87.6 %psum.14 = f32[3,4096]{1,0:T(4,128)S(1)} all-reduce(f32[3,4096]{1,0:T(4,128)S(1)} %bitcast.93), channel_id=1, replica_groups=mesh['grp'=8,'sub'=32] {'grp','sub'}, use_global_device_ids=true, to_apply=%region_5.6 | all-reduce | flops 12288 | bytes 98304 | tf_op jit(solution)/shard_map/psum | solution.py:82
  145.4 31.0 %all_gather.34 = f32[7,4096]{1,0:T(8,128)S(1)} all-gather(f32[7,128]{1,0:T(8,128)S(1)} %pad_maximum_fusion.8), channel_id=1, replica_groups=mesh['grp'=8,'sub'=32] {'sub'}, dimensions={1}, use_global_device_ids=true | all-gather | bytes 118272 | tf_op jit(solution)/shard_map/all_gather | solution.py:91
  176.4 1.9 fusion.26
  179.0 2.1 fusion.27
  181.2 32.3 %all_gather.35 = f32[7,4096]{1,0:T(8,128)S(1)} all-gather(f32[7,128]{1,0:T(8,128)S(1)} %pad_maximum_fusion.7), channel_id=1, replica_groups=mesh['grp'=8,'sub'=32] {'sub'}, dimensions={1}, use_global_device_ids=true | all-gather | bytes 118272 | tf_op jit(solution)/shard_map/all_gather | solution.py:91
  213.5 2.0 fusion.31
  216.2 2.2 fusion.11
  218.4 31.8 %all_gather.36 = f32[7,4096]{1,0:T(8,128)S(1)} all-gather(f32[7,128]{1,0:T(8,128)S(1)} %pad_maximum_fusion.6), channel_id=1, replica_groups=mesh['grp'=8,'sub'=32] {'sub'}, dimensions={1}, use_global_device_ids=true | all-gather | bytes 118272 | tf_op jit(solution)/shard_map/all_gather | solution.py:91
  250.2 2.0 fusion.34
  252.9 2.2 fusion.13
  255.1 33.7 %all_gather.37 = f32[7,4096]{1,0:T(8,128)S(1)} all-gather(f32[7,128]{1,0:T(8,128)S(1)} %pad_maximum_fusion.5), channel_id=1, replica_groups=mesh['grp'=8,'sub'=32] {'sub'}, dimensions={1}, use_global_device_ids=true | all-gather | bytes 118272 | tf_op jit(solution)/shard_map/all_gather | solution.py:91
  288.9 2.0 fusion.37
  291.5 2.2 fusion.15
  293.7 30.9 %all_gather.38 = f32[7,4096]{1,0:T(8,128)S(1)} all-gather(f32[7,128]{1,0:T(8,128)S(1)} %pad_maximum_fusion.4), channel_id=1, replica_groups=mesh['grp'=8,'sub'=32] {'sub'}, dimensions={1}, use_global_device_ids=true | all-gather | bytes 118272 | tf_op jit(solution)/shard_map/all_gather | solution.py:91
  324.6 2.0 fusion.40
  327.3 2.2 fusion.17
  329.5 33.5 %all_gather.39 = f32[7,4096]{1,0:T(8,128)S(1)} all-gather(f32[7,128]{1,0:T(8,128)S(1)} %pad_maximum_fusion.3), channel_id=1, replica_groups=mesh['grp'=8,'sub'=32] {'sub'}, dimensions={1}, use_global_device_ids=true | all-gather | bytes 118272 | tf_op jit(solution)/shard_map/all_gather | solution.py:91
  363.0 2.0 fusion.43
  365.7 2.2 fusion.19
  367.9 30.7 %all_gather.40 = f32[7,4096]{1,0:T(8,128)S(1)} all-gather(f32[7,128]{1,0:T(8,128)S(1)} %pad_maximum_fusion.2), channel_id=1, replica_groups=mesh['grp'=8,'sub'=32] {'sub'}, dimensions={1}, use_global_device_ids=true | all-gather | bytes 118272 | tf_op jit(solution)/shard_map/all_gather | solution.py:91
  398.6 2.0 fusion.46
  401.3 2.2 fusion.21
  403.5 33.4 %all_gather.41 = f32[7,4096]{1,0:T(8,128)S(1)} all-gather(f32[7,128]{1,0:T(8,128)S(1)} %pad_maximum_fusion.1), channel_id=1, replica_groups=mesh['grp'=8,'sub'=32] {'sub'}, dimensions={1}, use_global_device_ids=true | all-gather | bytes 118272 | tf_op jit(solution)/shard_map/all_gather | solution.py:91
  437.0 2.0 fusion.49
  439.6 2.2 fusion.23
  441.8 31.1 %all_gather.42 = f32[7,4096]{1,0:T(8,128)S(1)} all-gather(f32[7,128]{1,0:T(8,128)S(1)} %pad_maximum_fusion), channel_id=1, replica_groups=mesh['grp'=8,'sub'=32] {'sub'}, dimensions={1}, use_global_device_ids=true | all-gather | bytes 118272 | tf_op jit(solution)/shard_map/all_gather | solution.py:91
  473.0 2.0 fusion.52
  475.6 2.2 fusion.25
  477.9 36.5 %all_gather.43 = f32[4,4096]{1,0:T(4,128)S(1)} all-gather(f32[4,128]{1,0:T(4,128)S(1)} %pad_maximum_fusion.9), channel_id=1, replica_groups=mesh['grp'=8,'sub'=32] {'sub'}, dimensions={1}, use_global_device_ids=true | all-gather | bytes 67584 | tf_op jit(solution)/shard_map/all_gather | solution.py:79
  514.4 8.5 %while.9 = (s32[]{:T(128)}, f32[4,3,128]{2,1,0:T(4,128)S(1)}, f32[3,4096]{1,0:T(4,128)S(1)}, f32[4,3,128]{2,1,0:T(4,128)S(1)}, f32[1,4096]{1,0:T(1,128)S(1)}, /*index=5*/s32[]{:T(128)}) while((s32[]{:T(128)}, f32[4,3,128]{2,1,0:T(4,128)S(1)}, f32[3,4096]{1,0:T(4,128)S(1)}, f32[4,3,128]{2,1,0:T(4,128)S(1)}, f32[1,4096]{1,0:T(1,128)S(1)}, ...), condition=%wide.region_45.46_spmd, body=%wide.region_42.45_spmd.sunk | while | flops 11009666 | bytes 8515149 | solution.py:34
  514.5 0.9 fusion.72
  515.7 0.8 fusion.73
  516.6 0.9 fusion.72
  517.8 0.8 fusion.73
  518.7 0.9 fusion.72
  519.9 0.8 fusion.73
  520.8 0.9 fusion.72
  522.1 0.8 fusion.73
  523.0 8.5 %while.11 = (s32[]{:T(128)}, f32[4,3,128]{2,1,0:T(4,128)S(1)}, f32[3,4096]{1,0:T(4,128)S(1)}, f32[4,3,128]{2,1,0:T(4,128)S(1)}, f32[1,4096]{1,0:T(1,128)S(1)}, /*index=5*/s32[]{:T(128)}) while((s32[]{:T(128)}, f32[4,3,128]{2,1,0:T(4,128)S(1)}, f32[3,4096]{1,0:T(4,128)S(1)}, f32[4,3,128]{2,1,0:T(4,128)S(1)}, f32[1,4096]{1,0:T(1,128)S(1)}, ...), condition=%wide.region_54.55_spmd, body=%wide.region_51.54_spmd.sunk | while | flops 11009666 | bytes 8515149 | solution.py:34
  523.0 0.9 fusion.76
  525.1 0.9 fusion.76
  527.2 0.9 fusion.76
  529.4 0.9 fusion.76
  530.6 0.8 fusion.77
  532.1 10.4 %while.10 = (s32[]{:T(128)}, f32[4,3,1024]{2,1,0:T(4,128)S(1)}, f32[3,512]{1,0:T(4,128)S(1)}, f32[4,3,1024]{2,1,0:T(4,128)S(1)}, f32[512]{0:T(512)S(1)}, /*index=5*/s32[]{:T(128)}) while((s32[]{:T(128)}, f32[4,3,1024]{2,1,0:T(4,128)S(1)}, f32[3,512]{1,0:T(4,128)S(1)}, f32[4,3,1024]{2,1,0:T(4,128)S(1)}, f32[512]{0:T(512)S(1)}, ...), condition=%wide.region_49.50_spmd, body=%wide.region_46.49_spmd.sunk | while | flops 11006978 | bytes 8497229 | solution.py:34
  532.1 0.9 fusion.74
  533.4 1.2 fusion.75
  534.7 0.9 fusion.74
  536.0 1.2 fusion.75
  537.3 0.9 fusion.74
  538.6 1.2 fusion.75
  539.9 0.9 fusion.74
  541.2 1.2 fusion.75
  542.5 171.9 %psum.15 = f32[3,4096]{1,0:T(4,128)S(1)} all-reduce(f32[3,4096]{1,0:T(4,128)S(1)} %bitcast.92), channel_id=1, replica_groups=mesh['grp'=8,'sub'=32] {'grp','sub'}, use_global_device_ids=true, to_apply=%region_50.51 | all-reduce | flops 12288 | bytes 98304 | tf_op jit(solution)/shard_map/psum | solution.py:82
  (134 shorter events, 18.9 us)
Async XLA Ops:
  43.2 102.1 %copy-start.6 = (f32[3,128]{1,0:T(4,128)S(1)}, f32[3,128]{1,0:T(4,128)}, u32[]{:S(2)}) copy-start(f32[3,128]{1,0:T(4,128)} %param.16) | copy-start | bytes 4612
  43.2 102.1 %copy-start.3 = (f32[3,128]{1,0:T(4,128)S(1)}, f32[3,128]{1,0:T(4,128)}, u32[]{:S(2)}) copy-start(f32[3,128]{1,0:T(4,128)} %param.15) | copy-start | bytes 4612
  44.9 0.7 copy-start
  48.6 0.7 copy-start
  52.2 0.7 copy-start
  55.8 0.7 copy-start
  475.6 38.8 %copy-start.1 = (f32[3,512]{1,0:T(4,128)S(1)}, f32[3,512]{1,0:T(4,128)}, u32[]{:S(2)}) copy-start(f32[3,512]{1,0:T(4,128)} %get-tuple-element.607) | copy-start | bytes 18436
  477.8 36.6 %copy-start.5 = (f32[3,128]{1,0:T(4,128)}, f32[3,128]{1,0:T(4,128)S(1)}, u32[]{:S(2)}) copy-start(f32[3,128]{1,0:T(4,128)S(1)} %multiply_add_fusion.2) | copy-start | bytes 4612
  514.4 8.5 %copy-start.4 = (f32[3,512]{1,0:T(4,128)S(1)}, f32[3,512]{1,0:T(4,128)}, u32[]{:S(2)}) copy-start(f32[3,512]{1,0:T(4,128)} %param.19) | copy-start | bytes 18436
  542.5 172.5 %copy-start.2 = (f32[3,512]{1,0:T(4,128)}, f32[3,512]{1,0:T(4,128)S(1)}, u32[]{:S(2)}) copy-start(f32[3,512]{1,0:T(4,128)S(1)} %get-tuple-element.610) | copy-start | bytes 18436
where the time goes:
time: 725 us; the launch traced here: 715 us
  blocking collectives  625 us (86%)
  other arithmetic  86 us (12%)
    all_gather x9, blocking collectives, evaluate(): source_piece = lax.all_gather(sources, 'sub', axis=1, tiled=True)  288 us
    psum x2, blocking collectives, kick(): summed = lax.psum(partial_value, ('grp', 'sub'))  259 us
    all_gather x2, blocking collectives, kick(): gathered = lax.all_gather(stacked, 'sub', axis=1, tiled=True)  76.9 us
    reduce_sum x8, other arithmetic, rates_one_tile(): jnp.sum((closing - radial[None] * separation) * weight[None], axis=2)  17.5 us
    reduce_sum x16, other arithmetic, field_one_tile(): distance = jnp.sum(separation * separation, axis=0) + soften  17.3 us
    reduce_sum x16, other arithmetic, field_one_tile(): return jnp.sum(separation * weight[None], axis=2)  16.5 us
    reduce_sum x8, other arithmetic, rates_one_tile(): radial = 3.0 * jnp.sum(separation * closing, axis=0) / distance  16.4 us

commit v1 on v0

--- a/solution.py
+++ b/solution.py
@@ -79,7 +79,7 @@
         gathered = lax.all_gather(stacked, "sub", axis=1, tiled=True)
         galaxy_push = field(body_positions, gathered[:3], gathered[3], bridge_soft)
         partial_value = field(gathered[:3], body_positions, body_mass, bridge_soft)
-        summed = lax.psum(partial_value, ("grp", "sub"))
+        summed = lax.psum(lax.psum(partial_value, "sub"), "grp")
         cluster_pull = lax.dynamic_slice_in_dim(
             summed, lax.axis_index("sub") * star_count, star_count, 1
         )

time: 725 us -> 902 us (1.24)
  blocking collectives: 625 us -> 802 us
    psum x2 -> x4, blocking collectives: 259 us -> 437 us  [kick(): summed = lax.psum(lax.psum(partial_value, 'sub'), 'grp')]
where the time goes in v1:
time: 902 us; the launch traced here: 893 us
  blocking collectives  802 us (89%)
  other arithmetic  86 us (10%)
    psum x4, blocking collectives, kick(): summed = lax.psum(lax.psum(partial_value, 'sub'), 'grp')  437 us
    all_gather x9, blocking collectives, evaluate(): source_piece = lax.all_gather(sources, 'sub', axis=1, tiled=True)  288 us
    all_gather x2, blocking collectives, kick(): gathered = lax.all_gather(stacked, 'sub', axis=1, tiled=True)  76.4 us

profile of v1, /device:TPU:1, one launch (start us, length us, event | category | flops | bytes accessed | tf_op | source)
XLA Modules:
  0.0 892.7 jit_solution(12041371922638758788)
XLA Ops:
  2.0 40.5 %all_gather.33 = f32[4,4096]{1,0:T(4,128)S(1)} all-gather(f32[4,128]{1,0:T(4,128)S(1)} %pad_maximum_fusion.10), channel_id=1, replica_groups=mesh['grp'=8,'sub'=32] {'sub'}, dimensions={1}, use_global_device_ids=true | all-gather | bytes 67584 | tf_op jit(solution)/shard_map/all_gather | solution.py:79
  43.3 14.5 %while.8 = (s32[]{:T(128)}, f32[4,3,1024]{2,1,0:T(4,128)S(1)}, f32[3,512]{1,0:T(4,128)}, f32[4,3,1024]{2,1,0:T(4,128)S(1)}, f32[512]{0:T(512)S(1)}, /*index=5*/s32[]{:T(128)}) while((s32[]{:T(128)}, f32[4,3,1024]{2,1,0:T(4,128)S(1)}, f32[3,512]{1,0:T(4,128)}, f32[4,3,1024]{2,1,0:T(4,128)S(1)}, f32[512]{0:T(512)S(1)}, ...), condition=%wide.region_4.5_spmd, body=%wide.region_1.4_spmd.sunk | while | flops 11006978 | bytes 8521833 | solution.py:34
  43.3 1.6 fusion.70
  45.6 1.2 fusion.71
  46.9 1.6 fusion.70
  49.3 1.2 fusion.71
  50.5 1.6 fusion.70
  52.9 1.2 fusion.71
  54.2 1.6 fusion.70
  56.5 1.2 fusion.71
  57.8 112.9 %psum.28 = f32[3,4096]{1,0:T(4,128)S(1)} all-reduce(f32[3,4096]{1,0:T(4,128)S(1)} %bitcast.93), channel_id=1, replica_groups=mesh['grp'=8,'sub'=32] {'sub'}, use_global_device_ids=true, to_apply=%region_5.6 | all-reduce | flops 12288 | bytes 98304 | tf_op jit(solution)/shard_map/psum | solution.py:82
  170.7 61.4 %psum.29 = f32[3,4096]{1,0:T(4,128)S(1)} all-reduce(f32[3,4096]{1,0:T(4,128)S(1)} %psum.28), channel_id=1, replica_groups=mesh['grp'=8,'sub'=32] {'grp'}, use_global_device_ids=true, to_apply=%region_6.7 | all-reduce | flops 12288 | bytes 98304 | tf_op jit(solution)/shard_map/psum | solution.py:82
  232.2 30.2 %all_gather.34 = f32[7,4096]{1,0:T(8,128)S(1)} all-gather(f32[7,128]{1,0:T(8,128)S(1)} %pad_maximum_fusion.8), channel_id=1, replica_groups=mesh['grp'=8,'sub'=32] {'sub'}, dimensions={1}, use_global_device_ids=true | all-gather | bytes 118272 | tf_op jit(solution)/shard_map/all_gather | solution.py:91
  262.4 1.9 fusion.26
  264.9 2.1 fusion.27
  267.1 33.0 %all_gather.35 = f32[7,4096]{1,0:T(8,128)S(1)} all-gather(f32[7,128]{1,0:T(8,128)S(1)} %pad_maximum_fusion.7), channel_id=1, replica_groups=mesh['grp'=8,'sub'=32] {'sub'}, dimensions={1}, use_global_device_ids=true | all-gather | bytes 118272 | tf_op jit(solution)/shard_map/all_gather | solution.py:91
  300.2 2.0 fusion.31
  302.8 2.2 fusion.11
  305.1 31.8 %all_gather.36 = f32[7,4096]{1,0:T(8,128)S(1)} all-gather(f32[7,128]{1,0:T(8,128)S(1)} %pad_maximum_fusion.6), channel_id=1, replica_groups=mesh['grp'=8,'sub'=32] {'sub'}, dimensions={1}, use_global_device_ids=true | all-gather | bytes 118272 | tf_op jit(solution)/shard_map/all_gather | solution.py:91
  336.9 2.0 fusion.34
  339.5 2.2 fusion.13
  341.8 33.4 %all_gather.37 = f32[7,4096]{1,0:T(8,128)S(1)} all-gather(f32[7,128]{1,0:T(8,128)S(1)} %pad_maximum_fusion.5), channel_id=1, replica_groups=mesh['grp'=8,'sub'=32] {'sub'}, dimensions={1}, use_global_device_ids=true | all-gather | bytes 118272 | tf_op jit(solution)/shard_map/all_gather | solution.py:91
  375.2 2.0 fusion.37
  377.9 2.2 fusion.15
  380.1 30.8 %all_gather.38 = f32[7,4096]{1,0:T(8,128)S(1)} all-gather(f32[7,128]{1,0:T(8,128)S(1)} %pad_maximum_fusion.4), channel_id=1, replica_groups=mesh['grp'=8,'sub'=32] {'sub'}, dimensions={1}, use_global_device_ids=true | all-gather | bytes 118272 | tf_op jit(solution)/shard_map/all_gather | solution.py:91
  411.0 2.0 fusion.40
  413.6 2.2 fusion.17
  415.9 33.1 %all_gather.39 = f32[7,4096]{1,0:T(8,128)S(1)} all-gather(f32[7,128]{1,0:T(8,128)S(1)} %pad_maximum_fusion.3), channel_id=1, replica_groups=mesh['grp'=8,'sub'=32] {'sub'}, dimensions={1}, use_global_device_ids=true | all-gather | bytes 118272 | tf_op jit(solution)/shard_map/all_gather | solution.py:91
  449.0 2.0 fusion.43
  451.7 2.2 fusion.19
  453.9 30.5 %all_gather.40 = f32[7,4096]{1,0:T(8,128)S(1)} all-gather(f32[7,128]{1,0:T(8,128)S(1)} %pad_maximum_fusion.2), channel_id=1, replica_groups=mesh['grp'=8,'sub'=32] {'sub'}, dimensions={1}, use_global_device_ids=true | all-gather | bytes 118272 | tf_op jit(solution)/shard_map/all_gather | solution.py:91
  484.4 2.0 fusion.46
  487.0 2.2 fusion.21
  489.3 33.7 %all_gather.41 = f32[7,4096]{1,0:T(8,128)S(1)} all-gather(f32[7,128]{1,0:T(8,128)S(1)} %pad_maximum_fusion.1), channel_id=1, replica_groups=mesh['grp'=8,'sub'=32] {'sub'}, dimensions={1}, use_global_device_ids=true | all-gather | bytes 118272 | tf_op jit(solution)/shard_map/all_gather | solution.py:91
  523.0 2.0 fusion.49
  525.6 2.2 fusion.23
  527.8 31.8 %all_gather.42 = f32[7,4096]{1,0:T(8,128)S(1)} all-gather(f32[7,128]{1,0:T(8,128)S(1)} %pad_maximum_fusion), channel_id=1, replica_groups=mesh['grp'=8,'sub'=32] {'sub'}, dimensions={1}, use_global_device_ids=true | all-gather | bytes 118272 | tf_op jit(solution)/shard_map/all_gather | solution.py:91
  559.6 2.0 fusion.52
  562.3 2.2 fusion.25
  564.5 35.9 %all_gather.43 = f32[4,4096]{1,0:T(4,128)S(1)} all-gather(f32[4,128]{1,0:T(4,128)S(1)} %pad_maximum_fusion.9), channel_id=1, replica_groups=mesh['grp'=8,'sub'=32] {'sub'}, dimensions={1}, use_global_device_ids=true | all-gather | bytes 67584 | tf_op jit(solution)/shard_map/all_gather | solution.py:79
  600.6 8.5 while.9
  600.6 0.9 fusion.72
  602.7 0.9 fusion.72
  603.9 0.8 fusion.73
  604.8 0.9 fusion.72
  606.1 0.8 fusion.73
  607.0 0.9 fusion.72
  608.2 0.8 fusion.73
  609.1 8.5 while.11
  609.1 0.9 fusion.76
  611.3 0.9 fusion.76
  613.4 0.9 fusion.76
  615.5 0.9 fusion.76
  618.2 10.4 %while.10 = (s32[]{:T(128)}, f32[4,3,1024]{2,1,0:T(4,128)S(1)}, f32[3,512]{1,0:T(4,128)S(1)}, f32[4,3,1024]{2,1,0:T(4,128)S(1)}, f32[512]{0:T(512)S(1)}, /*index=5*/s32[]{:T(128)}) while((s32[]{:T(128)}, f32[4,3,1024]{2,1,0:T(4,128)S(1)}, f32[3,512]{1,0:T(4,128)S(1)}, f32[4,3,1024]{2,1,0:T(4,128)S(1)}, f32[512]{0:T(512)S(1)}, ...), condition=%wide.region_50.51_spmd, body=%wide.region_47.50_spmd.sunk | while | flops 11006978 | bytes 8497229 | solution.py:34
  618.2 0.9 fusion.74
  619.6 1.2 fusion.75
  620.8 0.9 fusion.74
  622.2 1.2 fusion.75
  623.4 0.9 fusion.74
  624.8 1.2 fusion.75
  626.0 0.9 fusion.74
  627.3 1.2 fusion.75
  628.6 112.2 %psum.30 = f32[3,4096]{1,0:T(4,128)S(1)} all-reduce(f32[3,4096]{1,0:T(4,128)S(1)} %bitcast.92), channel_id=1, replica_groups=mesh['grp'=8,'sub'=32] {'sub'}, use_global_device_ids=true, to_apply=%region_51.52 | all-reduce | flops 12288 | bytes 98304 | tf_op jit(solution)/shard_map/psum | solution.py:82
  740.8 150.9 %psum.31 = f32[3,4096]{1,0:T(4,128)S(1)} all-reduce(f32[3,4096]{1,0:T(4,128)S(1)} %psum.30), channel_id=1, replica_groups=mesh['grp'=8,'sub'=32] {'grp'}, use_global_device_ids=true, to_apply=%region_52.53 | all-reduce | flops 12288 | bytes 98304 | tf_op jit(solution)/shard_map/psum | solution.py:82
  (136 shorter events, 20.6 us)
Async XLA Ops:
  43.2 188.9 %copy-start.6 = (f32[3,128]{1,0:T(4,128)S(1)}, f32[3,128]{1,0:T(4,128)}, u32[]{:S(2)}) copy-start(f32[3,128]{1,0:T(4,128)} %param.16) | copy-start | bytes 4612
  43.2 188.9 %copy-start.3 = (f32[3,128]{1,0:T(4,128)S(1)}, f32[3,128]{1,0:T(4,128)}, u32[]{:S(2)}) copy-start(f32[3,128]{1,0:T(4,128)} %param.15) | copy-start | bytes 4612
  44.9 0.7 copy-start
  48.6 0.7 copy-start
  52.2 0.7 copy-start
  55.8 0.7 copy-start
  562.3 38.3 %copy-start.1 = (f32[3,512]{1,0:T(4,128)S(1)}, f32[3,512]{1,0:T(4,128)}, u32[]{:S(2)}) copy-start(f32[3,512]{1,0:T(4,128)} %get-tuple-element.607) | copy-start | bytes 18436
  564.5 36.1 %copy-start.5 = (f32[3,128]{1,0:T(4,128)}, f32[3,128]{1,0:T(4,128)S(1)}, u32[]{:S(2)}) copy-start(f32[3,128]{1,0:T(4,128)S(1)} %multiply_add_fusion.2) | copy-start | bytes 4612
  600.5 8.5 copy-start.4
  628.6 263.7 %copy-start.2 = (f32[3,512]{1,0:T(4,128)}, f32[3,512]{1,0:T(4,128)S(1)}, u32[]{:S(2)}) copy-start(f32[3,512]{1,0:T(4,128)S(1)} %get-tuple-element.610) | copy-start | bytes 18436
